TPU v7x, 32 devices: a whole 2x2x4 slice. The times are simulated.
32 devices in a mesh: dp: 16 (over z, x, core), head: 2 (over y).
Axes of the slice: x: 2, y: 2, z: 4, core: 2. Of those that a mesh axis runs over, the one named last changes fastest.
Arguments:
- tokens: bfloat16 [4, 8192, 768], P(None, 'dp'), may hold values from -6 to 6
- live: int32 [4, 8192], P(None, 'dp'), may hold values from 0 to 1, as said below
- bucket: int32 [4], replicated, may hold values from 64 to 512, as said below
- query_weight: bfloat16 [768, 768], P('dp', 'head'), may hold values from -0.21875 to 0.21875
- key_weight: bfloat16 [768, 768], P('dp', 'head'), may hold values from -0.21875 to 0.21875
- value_weight: bfloat16 [768, 768], P('dp', 'head'), may hold values from -0.21875 to 0.21875
- output_weight: bfloat16 [768, 768], P('head', 'dp'), may hold values from -0.875 to 0.875
- inner_weight: bfloat16 [768, 3072], P('dp', 'head'), may hold values from -0.21875 to 0.21875
- outer_weight: bfloat16 [3072, 768], P('head', 'dp'), may hold values from -0.109375 to 0.109375
- query_bias_vector: bfloat16 [768], P('head'), may hold values from -3 to 3
- value_bias_vector: bfloat16 [768], P('head'), may hold values from -3 to 3
- output_bias_vector: bfloat16 [768], replicated, may hold values from -3 to 3
- inner_bias_vector: bfloat16 [3072], P('head'), may hold values from -3 to 3
- outer_bias_vector: bfloat16 [768], replicated, may hold values from -3 to 3
- first_norm_scale: bfloat16 [768], replicated, may hold values from 0.099609375 to 1.8984375
- first_norm_bias: bfloat16 [768], replicated, may hold values from -2 to 2
- second_norm_scale: bfloat16 [768], replicated, may hold values from 0.099609375 to 1.8984375
- second_norm_bias: bfloat16 [768], replicated, may hold values from -2 to 2
- query_down_matrix: bfloat16 [768, 8], replicated, may hold values from -0.21875 to 0.21875
- value_down_matrix: bfloat16 [768, 8], replicated, may hold values from -0.21875 to 0.21875
- query_up_matrix: float32 [8, 768], P(None, 'head'), may hold values from -1.2 to 1.2
- value_up_matrix: float32 [8, 768], P(None, 'head'), may hold values from -1.2 to 1.2
- cotangent: bfloat16 [4, 8192, 768], P(None, 'dp'), may hold values from -6 to 6
Outputs:
- activations: bfloat16 [4, 8192, 768], P(None, 'dp')
- input_grad: bfloat16 [4, 8192, 768], P(None, 'dp')
- lora_query_grad: float32 [8, 768], P(None, 'head')
- lora_value_grad: float32 [8, 768], P(None, 'head')
Inputs may be any that keep to these rules, and one draw needn't show every extreme that they name: The four micro-batches take the bucket lengths 512, 256, 128 and 64, each once. The slots of micro-batch m form aligned items of bucket[m] slots; live is 1 on a prefix of each item longer than half of it and 0 after.
All inputs are finite; a program needn't handle non-finite values.
Results may differ from a plain program's by a relative error of at most 0.02.
Values may be sent and summed in bfloat16 or wider, within the bound.
No kernel may reach another device: no remote copies, remote signals or barrier semaphores. Data moves between devices by JAX's collectives and lax.ppermute only.
A program may use at most 192 MiB of HBM per device.

v0:
```python
import math
import jax
import jax.numpy as jnp
from jax import lax
from jax.sharding import PartitionSpec as P

HEAD_DIM = 64
ADAPTER_RANK = 8
ALPHA = 16
BUCKET_TOP = 512
eps_norm = 1e-05
masked_score = -1000000000.0
highest = lax.Precision.HIGHEST


def plain_dot(left, right):
    return jnp.dot(left, right, preferred_element_type=jnp.float32)


def back_dot(left, right):
    return lax.dot_general(
        left, right, (((1,), (1,)), ((), ())), preferred_element_type=jnp.float32
    )


def precise_backward(left, right):
    return lax.dot_general(
        left, right, (((1,), (1,)), ((), ())), precision=highest, preferred_element_type=jnp.float32
    )


def norm_rows(rows_in, gain, shift):
    center = rows_in - jnp.mean(rows_in, axis=-1, keepdims=True)
    spread = jnp.mean(center * center, axis=-1, keepdims=True)
    scaled = lax.rsqrt(spread + eps_norm)
    normalized_rows = center * scaled
    return (normalized_rows * gain + shift, normalized_rows, scaled)


def norm_back(grad_in, normalized_rows, scaled, gain):
    weighted = grad_in * gain
    return scaled * (
        weighted
        - jnp.mean(weighted, axis=-1, keepdims=True)
        - normalized_rows * jnp.mean(weighted * normalized_rows, axis=-1, keepdims=True)
    )


def gelu_slope(value_matrix):
    cdf_part = 0.5 * (1.0 + lax.erf(value_matrix / math.sqrt(2.0)))
    pdf_part = jnp.exp(-0.5 * value_matrix * value_matrix) / math.sqrt(2.0 * math.pi)
    return cdf_part + value_matrix * pdf_part


def collect(
    query_weight,
    key_weight,
    value_weight,
    inner_weight,
    output_weight,
    outer_weight,
    inner_bias_vector,
):
    rows_q, rows_k, rows_v, rows_in = (
        lax.all_gather(query_weight, "dp", axis=0, tiled=True),
        lax.all_gather(key_weight, "dp", axis=0, tiled=True),
        lax.all_gather(value_weight, "dp", axis=0, tiled=True),
        lax.all_gather(inner_weight, "dp", axis=0, tiled=True),
    )
    cols_out, cols_ffn = (
        lax.all_gather(output_weight, "dp", axis=1, tiled=True),
        lax.all_gather(outer_weight, "dp", axis=1, tiled=True),
    )
    return (
        rows_q,
        rows_k,
        rows_v,
        rows_in,
        cols_out,
        cols_ffn,
        inner_bias_vector.astype(jnp.float32),
    )


def adapter_gradient_sum(query_gradient, value_gradient):
    return lax.psum((query_gradient, value_gradient), "dp")


def shards(
    tokens,
    live,
    bucket,
    query_weight,
    key_weight,
    value_weight,
    output_weight,
    inner_weight,
    outer_weight,
    query_bias_vector,
    value_bias_vector,
    output_bias_vector,
    inner_bias_vector,
    outer_bias_vector,
    first_norm_scale,
    first_norm_bias,
    second_norm_scale,
    second_norm_bias,
    query_down_matrix,
    value_down_matrix,
    query_up_matrix,
    value_up_matrix,
    cotangent,
):
    micro_count, slots, model_width = tokens.shape
    width = query_weight.shape[1]
    group = width // HEAD_DIM
    blocks = slots // BUCKET_TOP
    adapter_multiplier = ALPHA / ADAPTER_RANK
    inverse = 1.0 / math.sqrt(HEAD_DIM)
    bias_q = query_bias_vector.astype(jnp.float32)
    bias_v = value_bias_vector.astype(jnp.float32)
    bias_out = output_bias_vector.astype(jnp.float32)
    bias_ffn = outer_bias_vector.astype(jnp.float32)
    gain_first = first_norm_scale.astype(jnp.float32)
    shift_first = first_norm_bias.astype(jnp.float32)
    gain_second = second_norm_scale.astype(jnp.float32)
    shift_second = second_norm_bias.astype(jnp.float32)
    down_q32 = query_down_matrix.astype(jnp.float32)
    down_v32 = value_down_matrix.astype(jnp.float32)
    query_total_sum = jnp.zeros(query_up_matrix.shape, jnp.float32)
    value_total_sum = jnp.zeros(value_up_matrix.shape, jnp.float32)
    positions = lax.iota(jnp.int32, BUCKET_TOP)
    outputs = []
    grads = []
    for section in range(micro_count):
        rows_q, rows_k, rows_v, rows_in, cols_out, cols_ffn, bias_in = collect(
            query_weight,
            key_weight,
            value_weight,
            inner_weight,
            output_weight,
            outer_weight,
            inner_bias_vector,
        )
        section_tokens = tokens[section]
        tokens_f32 = section_tokens.astype(jnp.float32)
        section_live = live[section]
        segment = positions // bucket[section]
        same_item = segment[:, None] == segment[None, :]
        live_keys = section_live.reshape(blocks, BUCKET_TOP) == 1
        permitted_mask = (same_item[None, :, :] & live_keys[:, None, :])[:, None, :, :]
        query_down_rows = plain_dot(section_tokens, query_down_matrix).astype(jnp.bfloat16)
        value_down_rows = plain_dot(section_tokens, value_down_matrix).astype(jnp.bfloat16)
        query_matrix = (
            plain_dot(section_tokens, rows_q)
            + bias_q
            + adapter_multiplier
            * jnp.dot(
                query_down_rows.astype(jnp.float32),
                query_up_matrix,
                precision=highest,
                preferred_element_type=jnp.float32,
            )
        )
        value_matrix = (
            plain_dot(section_tokens, rows_v)
            + bias_v
            + adapter_multiplier
            * jnp.dot(
                value_down_rows.astype(jnp.float32),
                value_up_matrix,
                precision=highest,
                preferred_element_type=jnp.float32,
            )
        )
        query_heads = query_matrix.astype(jnp.bfloat16).reshape(blocks, BUCKET_TOP, group, HEAD_DIM)
        key_heads = (
            plain_dot(section_tokens, rows_k)
            .astype(jnp.bfloat16)
            .reshape(blocks, BUCKET_TOP, group, HEAD_DIM)
        )
        value_heads = value_matrix.astype(jnp.bfloat16).reshape(blocks, BUCKET_TOP, group, HEAD_DIM)
        scores = (
            jnp.einsum(
                "nqhd,nkhd->nhqk", query_heads, key_heads, preferred_element_type=jnp.float32
            )
            * inverse
        )
        scores = jnp.where(permitted_mask, scores, masked_score)
        top_score = jnp.max(scores, axis=-1, keepdims=True)
        expo = jnp.exp(scores - top_score)
        probs = expo / jnp.sum(expo, axis=-1, keepdims=True)
        probs_low = probs.astype(jnp.bfloat16)
        context = jnp.einsum(
            "nhqk,nkhd->nqhd", probs_low, value_heads, preferred_element_type=jnp.float32
        )
        context_low = context.reshape(slots, width).astype(jnp.bfloat16)
        attended = lax.psum(plain_dot(context_low, cols_out).astype(jnp.bfloat16), "head").astype(
            jnp.float32
        )
        normed, normal_one, scaled_one = norm_rows(
            tokens_f32 + attended + bias_out, gain_first, shift_first
        )
        normed_low = normed.astype(jnp.bfloat16)
        pre_act = plain_dot(normed_low, rows_in) + bias_in
        activated = jax.nn.gelu(pre_act, approximate=False).astype(jnp.bfloat16)
        fed = lax.psum(plain_dot(activated, cols_ffn).astype(jnp.bfloat16), "head").astype(
            jnp.float32
        )
        out_float, normal_two, scaled_two = norm_rows(
            normed + fed + bias_ffn, gain_second, shift_second
        )
        outputs.append(out_float.astype(jnp.bfloat16))
        grad_out = cotangent[section].astype(jnp.float32) * section_live[:, None].astype(
            jnp.float32
        )
        grad_r_two = norm_back(grad_out, normal_two, scaled_two, gain_second)
        grad_act = back_dot(grad_r_two.astype(jnp.bfloat16), cols_ffn)
        grad_pre = (grad_act * gelu_slope(pre_act)).astype(jnp.bfloat16)
        grad_normed = grad_r_two + lax.psum(
            back_dot(grad_pre, rows_in).astype(jnp.bfloat16), "head"
        ).astype(jnp.float32)
        grad_r_one = norm_back(grad_normed, normal_one, scaled_one, gain_first)
        grad_one_low = grad_r_one.astype(jnp.bfloat16)
        grad_context = back_dot(grad_one_low, cols_out).astype(jnp.bfloat16)
        grad_context = grad_context.reshape(blocks, BUCKET_TOP, group, HEAD_DIM)
        grad_probs = jnp.einsum(
            "nqhd,nkhd->nhqk", grad_context, value_heads, preferred_element_type=jnp.float32
        )
        grad_value = jnp.einsum(
            "nhqk,nqhd->nkhd", probs_low, grad_context, preferred_element_type=jnp.float32
        )
        row_total = jnp.sum(probs * grad_probs, axis=-1, keepdims=True)
        grad_scores = (probs * (grad_probs - row_total)).astype(jnp.bfloat16)
        grad_query = (
            jnp.einsum(
                "nhqk,nkhd->nqhd", grad_scores, key_heads, preferred_element_type=jnp.float32
            )
            * inverse
        )
        grad_key = (
            jnp.einsum(
                "nhqk,nqhd->nkhd", grad_scores, query_heads, preferred_element_type=jnp.float32
            )
            * inverse
        )
        query_gradient_reduced = grad_query.reshape(slots, width).astype(jnp.bfloat16)
        grad_k_low = grad_key.reshape(slots, width).astype(jnp.bfloat16)
        value_gradient_reduced = grad_value.reshape(slots, width).astype(jnp.bfloat16)
        query_down_gradient = adapter_multiplier * precise_backward(
            query_gradient_reduced.astype(jnp.float32), query_up_matrix
        )
        value_down_gradient = adapter_multiplier * precise_backward(
            value_gradient_reduced.astype(jnp.float32), value_up_matrix
        )
        input_part = (
            back_dot(query_gradient_reduced, rows_q)
            + back_dot(grad_k_low, rows_k)
            + back_dot(value_gradient_reduced, rows_v)
        )
        input_part = (
            input_part
            + precise_backward(query_down_gradient, down_q32)
            + precise_backward(value_down_gradient, down_v32)
        )
        grad_tokens = grad_r_one + lax.psum(input_part.astype(jnp.bfloat16), "head").astype(
            jnp.float32
        )
        grads.append(grad_tokens.astype(jnp.bfloat16))
        query_adapter_term = adapter_multiplier * lax.dot_general(
            query_down_rows,
            query_gradient_reduced,
            (((0,), (0,)), ((), ())),
            preferred_element_type=jnp.float32,
        )
        value_adapter_term = adapter_multiplier * lax.dot_general(
            value_down_rows,
            value_gradient_reduced,
            (((0,), (0,)), ((), ())),
            preferred_element_type=jnp.float32,
        )
        query_summed_rows, value_summed_rows = adapter_gradient_sum(
            query_adapter_term, value_adapter_term
        )
        query_total_sum = query_total_sum + query_summed_rows
        value_total_sum = value_total_sum + value_summed_rows
    return (jnp.stack(outputs), jnp.stack(grads), query_total_sum, value_total_sum)


def solution(mesh):
    return jax.shard_map(
        shards,
        mesh=mesh,
        in_specs=(
            P(None, "dp", None),
            P(None, "dp"),
            P(),
            P("dp", "head"),
            P("dp", "head"),
            P("dp", "head"),
            P("head", "dp"),
            P("dp", "head"),
            P("head", "dp"),
            P("head"),
            P("head"),
            P(),
            P("head"),
            P(),
            P(),
            P(),
            P(),
            P(),
            P(),
            P(),
            P(None, "head"),
            P(None, "head"),
            P(None, "dp", None),
        ),
        out_specs=(P(None, "dp", None), P(None, "dp", None), P(None, "head"), P(None, "head")),
        check_vma=False,
    )
```

profile of v0, /device:TPU:0, one launch (start us, length us, event | category | flops | bytes accessed | tf_op | source)
XLA Modules:
  0.0 754.8 jit_solution(17762407008141377688)
XLA Ops:
  14.7 24.8 %all_gather.14 = bf16[768,384]{1,0:T(8,128)(2,1)S(1)} all-gather(bf16[48,384]{1,0:T(8,128)(2,1)S(1)} %copy-done.104), channel_id=1, replica_groups=mesh['dp'=16,'head'=2] {'dp'}, dimensions={0}, use_global_device_ids=true | all-gather | bytes 626688 | tf_op jit(solution)/shard_map/all_gather | solution.py:66
  42.1 19.1 %all_gather.12 = bf16[768,384]{1,0:T(8,128)(2,1)S(1)} all-gather(bf16[48,384]{1,0:T(8,128)(2,1)S(1)} %copy-done.105), channel_id=1, replica_groups=mesh['dp'=16,'head'=2] {'dp'}, dimensions={0}, use_global_device_ids=true | all-gather | bytes 626688 | tf_op jit(solution)/shard_map/all_gather | solution.py:67
  64.1 20.5 %all_gather.13 = bf16[768,384]{1,0:T(8,128)(2,1)S(1)} all-gather(bf16[48,384]{1,0:T(8,128)(2,1)S(1)} %copy-done.106), channel_id=1, replica_groups=mesh['dp'=16,'head'=2] {'dp'}, dimensions={0}, use_global_device_ids=true | all-gather | bytes 626688 | tf_op jit(solution)/shard_map/all_gather | solution.py:65
  94.9 20.9 %all_gather.15 = bf16[384,768]{0,1:T(8,128)(2,1)} all-gather(bf16[384,48]{0,1:T(8,128)(2,1)S(1)} %copy-done.107), channel_id=1, replica_groups=mesh['dp'=16,'head'=2] {'dp'}, dimensions={1}, use_global_device_ids=true | all-gather | bytes 626688 | tf_op jit(solution)/shard_map/all_gather | solution.py:71
  115.8 2.4 fusion.170
  118.3 2.4 fusion.164
  124.6 6.7 fusion.448
  131.3 3.6 fusion.172
  137.7 6.7 fusion.447
  144.3 3.5 fusion.190
  163.2 6.9 fusion.450
  170.2 3.5 fusion.178
  175.3 24.6 %all-reduce.24.cloned.1.call-done = (bf16[512,768]{1,0:T(8,128)(2,1)}, bf16[512,768]{1,0:T(8,128)(2,1)}) async-done(((bf16[512,768]{1,0:T(8,128)(2,1)}, bf16[512,768]{1,0:T(8,128)(2,1)}), (bf16[512,768]{1,0:T(8,128)(2,1)}, bf16[512,768]{1,0:T(8,128)(2,1)})) %all-reduce.24.cloned.1.call-update) | async-done | bytes 1572880 | tf_op jit(solution)/shard_map/psum | solution.py:198
  204.2 5.3 convolution_add_fusion
  209.5 3.4 convolution_add_fusion.3
  212.9 24.3 %all-gather.5.cloned.1.call-done = bf16[1536,768]{0,1:T(8,128)(2,1)} async-done(((bf16[1536,48]{0,1:T(8,128)(2,1)}), bf16[1536,768]{0,1:T(8,128)(2,1)}) %all-gather.5.cloned.1.call-update) | async-done | bytes 2359312 | tf_op jit(solution)/shard_map/all_gather | solution.py:72
  237.3 11.2 %fusion.141 = bf16[512,768]{1,0:T(8,128)(2,1)} fusion(bf16[1536,768]{0,1:T(8,128)(2,1)} %all-gather.5.cloned.1.call-done, f32[512,1536]{1,0:T(8,128)} %convolution_add_fusion), kind=kOutput, calls=%fused_computation.257 | convolution fusion | flops 1259470848 | bytes 6291456 | tf_op jit(solution)/shard_map/dot_general | solution.py:17
  248.5 8.8 %fusion.132 = bf16[512,768]{1,0:T(8,128)(2,1)} fusion(bf16[1536,768]{0,1:T(8,128)(2,1)S(1)} %copy-done.159, f32[512,1536]{1,0:T(8,128)S(1)} %copy-done.161), kind=kOutput, calls=%fused_computation.254 | convolution fusion | flops 1259470848 | bytes 6291456 | tf_op jit(solution)/shard_map/dot_general | solution.py:17
  263.0 6.8 fusion.449
  269.9 3.6 fusion.184
  275.0 32.6 %all-reduce.22.cloned.1.call-done = (bf16[512,768]{1,0:T(8,128)(2,1)}, bf16[512,768]{1,0:T(8,128)(2,1)}) async-done(((bf16[512,768]{1,0:T(8,128)(2,1)}, bf16[512,768]{1,0:T(8,128)(2,1)}), (bf16[512,768]{1,0:T(8,128)(2,1)}, bf16[512,768]{1,0:T(8,128)(2,1)})) %all-reduce.22.cloned.1.call-update) | async-done | bytes 1572880 | tf_op jit(solution)/shard_map/psum | solution.py:207
  307.7 3.0 fusion.444
  314.1 2.8 fusion.85
  317.0 7.4 convolution_convert_fusion.3
  324.4 7.4 convolution_convert_fusion
  332.0 86.3 %all-reduce.20.cloned.1.call-done = (bf16[512,768]{1,0:T(8,128)(2,1)}, bf16[512,768]{1,0:T(8,128)(2,1)}, bf16[512,768]{1,0:T(8,128)(2,1)}, bf16[512,768]{1,0:T(8,128)(2,1)}) async-done(((bf16[512,768]{1,0:T(8,128)(2,1)}, bf16[512,768]{1,0:T(8,128)(2,1)}, bf16[512,768]{1,0:T(8,128)(2,1)}, bf16[512,768]{1,0:T(8,128)(2,1)}), (bf16[512,768]{1,0:T(8,128)(2,1)}, bf16[512,768]{1,0:T(8,128)(2,1)}, ...) | async-done | bytes 3145744 | tf_op jit(solution)/shard_map/psum | solution.py:198
  418.3 4.4 multiply_reduce_fusion.7
  426.1 8.8 %fusion.138 = bf16[512,768]{1,0:T(8,128)(2,1)} fusion(bf16[1536,768]{0,1:T(8,128)(2,1)S(1)} %copy-done.160, f32[512,1536]{1,0:T(8,128)S(1)} %convolution_add_fusion.1), kind=kOutput, calls=%fused_computation.256 | convolution fusion | flops 1259470848 | bytes 6291456 | tf_op jit(solution)/shard_map/dot_general | solution.py:17
  438.1 9.0 %fusion.135 = bf16[512,768]{1,0:T(8,128)(2,1)} fusion(bf16[1536,768]{0,1:T(8,128)(2,1)S(1)} %copy-done.160, f32[512,1536]{1,0:T(8,128)S(1)} %convolution_add_fusion.2), kind=kOutput, calls=%fused_computation.255 | convolution fusion | flops 1259470848 | bytes 6291456 | tf_op jit(solution)/shard_map/dot_general | solution.py:17
  447.2 51.8 %all-reduce.18.cloned.1.call-done = (bf16[512,768]{1,0:T(8,128)(2,1)}, bf16[512,768]{1,0:T(8,128)(2,1)}) async-done(((bf16[512,768]{1,0:T(8,128)(2,1)}, bf16[512,768]{1,0:T(8,128)(2,1)}), (bf16[512,768]{1,0:T(8,128)(2,1)}, bf16[512,768]{1,0:T(8,128)(2,1)})) %all-reduce.18.cloned.1.call-update) | async-done | bytes 1572880 | tf_op jit(solution)/shard_map/psum | solution.py:207
  499.0 3.0 fusion.442
  505.4 2.9 fusion.92
  508.3 7.4 convolution_convert_fusion.2
  515.7 7.4 convolution_convert_fusion.1
  524.3 50.6 %all-reduce.16.cloned.1.call-done = (bf16[512,768]{1,0:T(8,128)(2,1)}, bf16[512,768]{1,0:T(8,128)(2,1)}) async-done(((bf16[512,768]{1,0:T(8,128)(2,1)}, bf16[512,768]{1,0:T(8,128)(2,1)}), (bf16[512,768]{1,0:T(8,128)(2,1)}, bf16[512,768]{1,0:T(8,128)(2,1)})) %all-reduce.16.cloned.1.call-update) | async-done | bytes 1572880 | tf_op jit(solution)/shard_map/psum | solution.py:220
  575.0 4.4 multiply_reduce_fusion.6
  579.5 2.9 subtract_multiply_fusion.1
  584.3 3.6 multiply_reduce_fusion
  587.9 3.9 multiply_convert_fusion
  597.9 3.6 multiply_reduce_fusion.1
  601.5 3.9 multiply_convert_fusion.1
  613.7 3.8 multiply_reduce_fusion.2
  617.5 3.9 multiply_convert_fusion.2
  626.7 3.7 multiply_reduce_fusion.3
  630.4 3.9 multiply_convert_fusion.3
  656.3 3.1 pad_maximum_fusion
  661.5 61.2 %all-reduce = (f32[8,384]{1,0:T(8,128)}, f32[8,384]{1,0:T(8,128)}) all-reduce(f32[8,384]{1,0:T(8,128)S(1)} %fusion.201, f32[8,384]{1,0:T(8,128)S(1)} %fusion.200), channel_id=1, replica_groups=mesh['dp'=16,'head'=2] {'dp'}, use_global_device_ids=true, to_apply=%region_60.61 | all-reduce | flops 6144 | bytes 49152 | tf_op jit(solution)/shard_map/psum | solution.py:86
  722.7 18.7 %all-reduce.14.cloned.1.call-done = (bf16[512,768]{1,0:T(8,128)(2,1)}, bf16[512,768]{1,0:T(8,128)(2,1)}, bf16[512,768]{1,0:T(8,128)(2,1)}, bf16[512,768]{1,0:T(8,128)(2,1)}) async-done(((bf16[512,768]{1,0:T(8,128)(2,1)}, bf16[512,768]{1,0:T(8,128)(2,1)}, bf16[512,768]{1,0:T(8,128)(2,1)}, bf16[512,768]{1,0:T(8,128)(2,1)}), (bf16[512,768]{1,0:T(8,128)(2,1)}, bf16[512,768]{1,0:T(8,128)(2,1)}, ...) | async-done | bytes 3145744 | tf_op jit(solution)/shard_map/psum | solution.py:266
  (515 shorter events, 119.7 us)
Async XLA Ops:
  8.0 31.5 %copy-start.1 = (bf16[4,512,768]{2,1,0:T(8,128)(2,1)S(1)}, bf16[4,512,768]{2,1,0:T(8,128)(2,1)}, u32[]{:S(2)}) copy-start(bf16[4,512,768]{2,1,0:T(8,128)(2,1)} %param.23) | copy-start | bytes 9437188
  8.0 191.8 %all-reduce.24.cloned.1.call-start = ((), (), s32[]{:S(2)}) async-start(), calls=%async_computation.7 | async-start | bytes 3145728 | tf_op jit(solution)/shard_map/psum | solution.py:198
  9.7 111.0 %copy-start.111 = (bf16[512,8]{0,1:T(8,128)(2,1)}, bf16[512,8]{0,1:T(8,128)(2,1)S(1)}, u32[]{:S(2)}) copy-start(bf16[512,8]{0,1:T(8,128)(2,1)S(1)} %convolution_convert_fusion.16) | copy-start | bytes 24580
  11.7 30.4 %copy-start.155 = (bf16[384]{0:T(512)(128)(2,1)S(1)}, bf16[384]{0:T(512)(128)(2,1)}, u32[]{:S(2)}) copy-start(bf16[384]{0:T(512)(128)(2,1)} %param.33) | copy-start | bytes 2308
  11.8 30.4 %copy-start.105 = (bf16[48,384]{1,0:T(8,128)(2,1)S(1)}, bf16[48,384]{1,0:T(8,128)(2,1)}, u32[]{:S(2)}) copy-start(bf16[48,384]{1,0:T(8,128)(2,1)} %param.28) | copy-start | bytes 110596
  13.2 102.6 %copy-start.113 = (bf16[512,8]{0,1:T(8,128)(2,1)}, bf16[512,8]{0,1:T(8,128)(2,1)S(1)}, u32[]{:S(2)}) copy-start(bf16[512,8]{0,1:T(8,128)(2,1)S(1)} %convolution_convert_fusion.17) | copy-start | bytes 24580
  14.7 103.6 %copy-start.109 = (bf16[512,8]{0,1:T(8,128)(2,1)}, bf16[512,8]{0,1:T(8,128)(2,1)S(1)}, u32[]{:S(2)}) copy-start(bf16[512,8]{0,1:T(8,128)(2,1)S(1)} %convolution_convert_fusion.23) | copy-start | bytes 24580
  39.5 23.1 %copy-start.15 = (bf16[768,384]{1,0:T(8,128)(2,1)}, bf16[768,384]{1,0:T(8,128)(2,1)S(1)}, u32[]{:S(2)}) copy-start(bf16[768,384]{1,0:T(8,128)(2,1)S(1)} %all_gather.14) | copy-start | bytes 1769476
  40.8 23.2 %copy-start.156 = (bf16[384]{0:T(512)(128)(2,1)S(1)}, bf16[384]{0:T(512)(128)(2,1)}, u32[]{:S(2)}) copy-start(bf16[384]{0:T(512)(128)(2,1)} %param.32) | copy-start | bytes 2308
  40.8 23.2 %copy-start.106 = (bf16[48,384]{1,0:T(8,128)(2,1)S(1)}, bf16[48,384]{1,0:T(8,128)(2,1)}, u32[]{:S(2)}) copy-start(bf16[48,384]{1,0:T(8,128)(2,1)} %param.26) | copy-start | bytes 110596
  42.1 43.8 %copy-start.149 = (f32[384]{0:T(512)}, f32[384]{0:T(512)S(1)}, u32[]{:S(2)}) copy-start(f32[384]{0:T(512)S(1)} %convert_element_type.605) | copy-start | bytes 4612
  61.2 24.8 %copy-start.21 = (bf16[768,384]{1,0:T(8,128)(2,1)}, bf16[768,384]{1,0:T(8,128)(2,1)S(1)}, u32[]{:S(2)}) copy-start(bf16[768,384]{1,0:T(8,128)(2,1)S(1)} %all_gather.12) | copy-start | bytes 1769476
  62.6 24.8 %copy-start.144 = (s32[4]{0:T(128)S(1)}, s32[4]{0:T(128)}, u32[]{:S(2)}) copy-start(s32[4]{0:T(128)} %param.25) | copy-start | bytes 52
  62.6 31.7 %copy-start.123 = (s32[4,512]{1,0:T(4,128)S(1)}, s32[4,512]{1,0:T(4,128)}, u32[]{:S(2)}) copy-start(s32[4,512]{1,0:T(4,128)} %param.24) | copy-start | bytes 24580
  62.6 32.3 %copy-start.107 = (bf16[384,48]{0,1:T(8,128)(2,1)S(1)}, bf16[384,48]{0,1:T(8,128)(2,1)}, u32[]{:S(2)}) copy-start(bf16[384,48]{0,1:T(8,128)(2,1)} %param.29) | copy-start | bytes 110596
  64.1 51.8 %copy-start.76 = (f32[8,384]{1,0:T(8,128)S(1)}, f32[8,384]{1,0:T(8,128)}, u32[]{:S(2)}) copy-start(f32[8,384]{1,0:T(8,128)} %param.44) | copy-start | bytes 36868
  64.1 24.0 %copy-start.151 = (f32[384]{0:T(512)}, f32[384]{0:T(512)S(1)}, u32[]{:S(2)}) copy-start(f32[384]{0:T(512)S(1)} %convert_element_type.608) | copy-start | bytes 4612
  86.0 34.7 %copy-start.73 = (f32[8,384]{1,0:T(8,128)S(1)}, f32[8,384]{1,0:T(8,128)}, u32[]{:S(2)}) copy-start(f32[8,384]{1,0:T(8,128)} %param.43) | copy-start | bytes 36868
  90.6 30.1 %copy-start.69 = (f32[512,384]{0,1:T(8,128)S(1)}, f32[512,384]{0,1:T(8,128)}, u32[]{:S(2)}) copy-start(f32[512,384]{0,1:T(8,128)} %convolution_add_fusion.4) | copy-start | bytes 2359300
  90.6 31.4 %copy-start.68 = (f32[512,384]{0,1:T(8,128)S(1)}, f32[512,384]{0,1:T(8,128)}, u32[]{:S(2)}) copy-start(f32[512,384]{0,1:T(8,128)} %convolution_add_fusion.10) | copy-start | bytes 2359300
  149.4 54.7 %all-gather.3.cloned.1.call-start = ((), (), s32[]{:S(2)}) async-start(), calls=%async_computation | async-start | bytes 2506752 | tf_op jit(solution)/shard_map/all_gather | solution.py:68
  150.0 87.2 %all-gather.5.cloned.1.call-start = ((), (), s32[]{:S(2)}) async-start(), calls=%async_computation.1 | async-start | bytes 2506752 | tf_op jit(solution)/shard_map/all_gather | solution.py:72
  150.6 157.0 %all-reduce.22.cloned.1.call-start = ((), (), s32[]{:S(2)}) async-start(), calls=%async_computation.6 | async-start | bytes 3145728 | tf_op jit(solution)/shard_map/psum | solution.py:207
  151.1 10.2 %copy-start.115 = (bf16[512,8]{0,1:T(8,128)(2,1)}, bf16[512,8]{0,1:T(8,128)(2,1)S(1)}, u32[]{:S(2)}) copy-start(bf16[512,8]{0,1:T(8,128)(2,1)S(1)} %convolution_convert_fusion.18) | copy-start | bytes 24580
  151.5 11.2 %copy-start.117 = (bf16[512,8]{0,1:T(8,128)(2,1)}, bf16[512,8]{0,1:T(8,128)(2,1)S(1)}, u32[]{:S(2)}) copy-start(bf16[512,8]{0,1:T(8,128)(2,1)S(1)} %convolution_convert_fusion.20) | copy-start | bytes 24580
  237.3 11.2 %copy-start.159 = (bf16[1536,768]{0,1:T(8,128)(2,1)S(1)}, bf16[1536,768]{0,1:T(8,128)(2,1)}, u32[]{:S(2)}) copy-start(bf16[1536,768]{0,1:T(8,128)(2,1)} %all-gather.5.cloned.1.call-done) | copy-start | bytes 7077892
  237.3 11.2 %copy-start.161 = (f32[512,1536]{1,0:T(8,128)S(1)}, f32[512,1536]{1,0:T(8,128)}, u32[]{:S(2)}) copy-start(f32[512,1536]{1,0:T(8,128)} %convolution_add_fusion.3) | copy-start | bytes 9437188
  248.5 14.6 %copy-start.63 = (bf16[512,384]{0,1:T(8,128)(2,1)S(1)}, bf16[512,384]{0,1:T(8,128)(2,1)}, u32[]{:S(2)}) copy-start(bf16[512,384]{0,1:T(8,128)(2,1)} %fusion.169) | copy-start | bytes 1179652
  257.3 161.0 %all-reduce.20.cloned.1.call-start = ((), (), s32[]{:S(2)}) async-start(), calls=%async_computation.5 | async-start | bytes 6291456 | tf_op jit(solution)/shard_map/psum | solution.py:198
  269.8 37.8 %copy-start.88 = (f32[768]{0:T(1024)S(1)}, f32[768]{0:T(1024)}, u32[]{:S(2)}) copy-start(f32[768]{0:T(1024)} %convert_element_type.620) | copy-start | bytes 9220
  269.8 37.8 %copy-start.94 = (f32[512]{0:T(512)S(1)}, f32[512]{0:T(512)}, u32[]{:S(2)}) copy-start(f32[512]{0:T(512)} %copy-done.93) | copy-start | bytes 6148
  269.8 37.8 %copy-start.98 = (f32[512]{0:T(512)S(1)}, f32[512]{0:T(512)}, u32[]{:S(2)}) copy-start(f32[512]{0:T(512)} %copy-done.97) | copy-start | bytes 6148
  269.8 37.8 %copy-start.102 = (f32[768]{0:T(1024)S(1)}, f32[768]{0:T(1024)}, u32[]{:S(2)}) copy-start(f32[768]{0:T(1024)} %convert_element_type.621) | copy-start | bytes 9220
  269.8 37.8 %copy-start.103 = (f32[768]{0:T(1024)S(1)}, f32[768]{0:T(1024)}, u32[]{:S(2)}) copy-start(f32[768]{0:T(1024)} %convert_element_type.627) | copy-start | bytes 9220
  269.9 37.8 %copy-start.125 = (f32[512]{0:T(512)S(1)}, f32[512]{0:T(512)}, u32[]{:S(2)}) copy-start(f32[512]{0:T(512)} %copy-done.124) | copy-start | bytes 6148
  269.9 37.8 %copy-start.128 = (f32[512]{0:T(512)S(1)}, f32[512]{0:T(512)}, u32[]{:S(2)}) copy-start(f32[512]{0:T(512)} %copy-done.127) | copy-start | bytes 6148
  331.8 167.2 %all-reduce.18.cloned.1.call-start = ((), (), s32[]{:S(2)}) async-start(), calls=%async_computation.4 | async-start | bytes 3145728 | tf_op jit(solution)/shard_map/psum | solution.py:207
  422.8 152.2 %copy-start.95 = (f32[512]{0:T(512)}, f32[512]{0:T(512)S(1)}, u32[]{:S(2)}) copy-start(f32[512]{0:T(512)S(1)} %broadcast_multiply_fusion.21) | copy-start | bytes 6148
  423.7 151.2 %copy-start.129 = (f32[512]{0:T(512)}, f32[512]{0:T(512)S(1)}, u32[]{:S(2)}) copy-start(f32[512]{0:T(512)S(1)} %add_rsqrt_fusion.5) | copy-start | bytes 6148
  447.2 127.7 %all-reduce.16.cloned.1.call-start = ((), (), s32[]{:S(2)}) async-start(), calls=%async_computation.3 | async-start | bytes 3145728 | tf_op jit(solution)/shard_map/psum | solution.py:220
  523.1 218.3 %all-reduce.14.cloned.1.call-start = ((), (), s32[]{:S(2)}) async-start(), calls=%async_computation.2 | async-start | bytes 6291456 | tf_op jit(solution)/shard_map/psum | solution.py:266
  582.4 13.8 %copy-start.24 = (f32[512,768]{1,0:T(8,128)}, f32[512,768]{1,0:T(8,128)S(1)}, u32[]{:S(2)}) copy-start(f32[512,768]{1,0:T(8,128)S(1)} %get-tuple-element.66) | copy-start | bytes 4718596
  584.3 64.1 %copy-start.45 = (bf16[6,64,512]{2,1,0:T(8,128)(2,1)}, bf16[6,64,512]{2,1,0:T(8,128)(2,1)S(1)}, u32[]{:S(2)}) copy-start(bf16[6,64,512]{2,1,0:T(8,128)(2,1)S(1)} %fusion.193) | copy-start | bytes 1179652
  597.9 52.1 %copy-start.47 = (bf16[6,64,512]{2,1,0:T(8,128)(2,1)}, bf16[6,64,512]{2,1,0:T(8,128)(2,1)S(1)}, u32[]{:S(2)}) copy-start(bf16[6,64,512]{2,1,0:T(8,128)(2,1)S(1)} %fusion.187) | copy-start | bytes 1179652
  611.9 13.2 %copy-start.29 = (f32[512,768]{1,0:T(8,128)}, f32[512,768]{1,0:T(8,128)S(1)}, u32[]{:S(2)}) copy-start(f32[512,768]{1,0:T(8,128)S(1)} %get-tuple-element.64) | copy-start | bytes 4718596
  613.7 37.8 %copy-start.49 = (bf16[6,64,512]{2,1,0:T(8,128)(2,1)}, bf16[6,64,512]{2,1,0:T(8,128)(2,1)S(1)}, u32[]{:S(2)}) copy-start(bf16[6,64,512]{2,1,0:T(8,128)(2,1)S(1)} %fusion.181) | copy-start | bytes 1179652
  626.7 26.4 %copy-start.43 = (bf16[6,64,512]{2,1,0:T(8,128)(2,1)}, bf16[6,64,512]{2,1,0:T(8,128)(2,1)S(1)}, u32[]{:S(2)}) copy-start(bf16[6,64,512]{2,1,0:T(8,128)(2,1)S(1)} %fusion.175) | copy-start | bytes 1179652
  659.4 81.9 %copy-start.30 = (f32[512,768]{1,0:T(8,128)S(1)}, f32[512,768]{1,0:T(8,128)}, u32[]{:S(2)}) copy-start(f32[512,768]{1,0:T(8,128)} %copy-done.29) | copy-start | bytes 4718596
  (132 other events, 466.7 us)
Sparse Core Ops, SparseCore 0:
  149.6 50.2 all-reduce.23
  257.4 50.1 all-reduce.21
  331.9 86.3 all-reduce.19
  447.3 51.6 all-reduce.17
  523.2 51.6 all-reduce.15
  655.0 86.3 all-reduce.13
Sparse Core Ops, SparseCore 1:
  152.5 41.1 all-gather.2
  196.0 41.2 all-gather.4
where the time goes:
time: 760 us; the launch traced here: 755 us
  waiting for transfers between devices  290 us (38%)
  matrix products  215 us (28%)
  blocking collectives  146 us (19%)
  other arithmetic  73.9 us (10%)
  between operations  20.5 us (3%)
  local copies, waits for them, and re-layouts  8.15 us (1%)
    psum x2, waiting for transfers between devices, shards(): lax.psum(plain_dot(context_low, cols_out).astype(jnp.bfloat16), 'head')  111 us
    psum x2, waiting for transfers between devices, shards(): lax.psum(plain_dot(activated, cols_ffn).astype(jnp.bfloat16), 'head')  84.4 us
    dot_general x32, matrix products, plain_dot(): return jnp.dot(left, right, preferred_element_type=jnp.float32)  76.4 us
    psum x1, blocking collectives, adapter_gradient_sum(): return lax.psum((query_gradient, value_gradient), 'dp')  61.2 us
    psum x1, waiting for transfers between devices, shards(): lax.psum(back_dot(grad_pre, rows_in).astype(jnp.bfloat16), 'head')  50.6 us
    dot_general x20, matrix products, back_dot(): lax.dot_general(left, right, (((1,), (1,)), ((), ())), preferred_element_...  42.8 us
    sub x4, matrix products, shards(): expo = jnp.exp(scores - top_score)  27.1 us
    all_gather x1, blocking collectives, collect(): lax.all_gather(key_weight, 'dp', axis=0, tiled=True)  24.8 us
  transfers between devices with their start and end apart: 8, of which 7 were waited for; matrix products, arithmetic and copies ran while one was open for 8% of the time, Pallas kernels for 0%

commit v1 on v0

--- a/solution.py
+++ b/solution.py
@@ -1,3 +1,4 @@
+import functools
 import math
 import jax
 import jax.numpy as jnp
@@ -11,6 +12,32 @@
 eps_norm = 1e-05
 masked_score = -1000000000.0
 highest = lax.Precision.HIGHEST
+
+
+def refer_the_lanes(in_array, lane_axis):
+    all_values = lax.psum(1, axis_name=lane_axis)
+    current_block, fresh, z1 = (all_values, lax.axis_index(lane_axis), in_array.shape[0])
+    log = [num * current_block if pp == 0 else num for pp, num in enumerate(in_array.shape)]
+    oldest = jnp.zeros(log, in_array.dtype)
+    w1 = lax.dynamic_update_slice_in_dim(oldest, in_array, fresh * z1, axis=0)
+    t_next = r_now = in_array
+    for it in range(1, current_block // 2 + 1):
+        t_next = lax.ppermute(
+            t_next,
+            axis_name=lane_axis,
+            perm=list(map(lambda pp: (pp, (pp + 1) % current_block), range(current_block))),
+        )
+        w1 = lax.dynamic_update_slice_in_dim(w1, t_next, (fresh - it) % current_block * z1, axis=0)
+        if 2 * it < current_block:
+            lower = list(map(lambda pp: (pp, (pp - 1) % current_block), range(current_block)))
+            r_now = lax.ppermute(r_now, axis_name=lane_axis, perm=lower)
+            w1 = lax.dynamic_update_slice_in_dim(
+                w1, r_now, (fresh + it) % current_block * z1, axis=0
+            )
+    return w1
+
+
+seats_all_work = functools.partial(refer_the_lanes, lane_axis="dp")
 
 
 def plain_dot(left, right):
@@ -63,7 +90,7 @@
 ):
     rows_q, rows_k, rows_v, rows_in = (
         lax.all_gather(query_weight, "dp", axis=0, tiled=True),
-        lax.all_gather(key_weight, "dp", axis=0, tiled=True),
+        seats_all_work(key_weight),
         lax.all_gather(value_weight, "dp", axis=0, tiled=True),
         lax.all_gather(inner_weight, "dp", axis=0, tiled=True),
     )

time: 760 us -> 813 us (1.070)
  starting transfers between devices: 1.08 us -> 34.1 us
  matrix products: 215 us -> 239 us
  blocking collectives: 146 us -> 123 us
  local copies, waits for them, and re-layouts: 8.15 us -> 25.2 us
    ppermute x0 -> x15, starting transfers between devices: none -> 32.6 us  [the longest x7 31.5 us: refer_the_lanes(): r_now = lax.ppermute(r_now, axis_name=lane_axis, perm=lower)]
    all_gather x1 -> x0, blocking collectives: 24.8 us -> none  [collect(): lax.all_gather(key_weight, 'dp', axis=0, tiled=True)]
    dynamic_update_slice x0 -> x16, local copies, waits for them, and re-layouts: none -> 12.2 us  [the longest x8 5.67 us: refer_the_lanes(): lax.dynamic_update_slice_in_dim(w1, t_next, (fresh - it) % current_block...]
    psum x2, waiting for transfers between devices: 111 us -> 102 us  [shards(): lax.psum(plain_dot(context_low, cols_out).astype(jnp.bfloat16), 'head')]
  transfers between devices with their start and end apart: 8 -> 23, of which waited for: 7 -> 15; matrix products, arithmetic and copies ran while one was open for 8% -> 13% of each run, Pallas kernels for 0% -> 0%
where the time goes in v1:
time: 813 us; the launch traced here: 806 us
  waiting for transfers between devices  291 us (36%)
  matrix products  239 us (29%)
  blocking collectives  123 us (15%)
  other arithmetic  73 us (9%)
  starting transfers between devices  34.1 us (4%)
  local copies, waits for them, and re-layouts  25.2 us (3%)
  between operations  20.4 us (3%)
    psum x2, waiting for transfers between devices, shards(): lax.psum(plain_dot(context_low, cols_out).astype(jnp.bfloat16), 'head')  102 us
    psum x2, waiting for transfers between devices, shards(): lax.psum(plain_dot(activated, cols_ffn).astype(jnp.bfloat16), 'head')  87.1 us
    dot_general x32, matrix products, plain_dot(): return jnp.dot(left, right, preferred_element_type=jnp.float32)  81.7 us
    psum x1, blocking collectives, adapter_gradient_sum(): return lax.psum((query_gradient, value_gradient), 'dp')  61.2 us
    psum x1, waiting for transfers between devices, shards(): lax.psum(back_dot(grad_pre, rows_in).astype(jnp.bfloat16), 'head')  51.7 us
    dot_general x20, matrix products, back_dot(): lax.dot_general(left, right, (((1,), (1,)), ((), ())), preferred_element_...  50.9 us
    ppermute x7, starting transfers between devices, refer_the_lanes(): r_now = lax.ppermute(r_now, axis_name=lane_axis, perm=lower)  31.5 us
    sub x4, matrix products, shards(): expo = jnp.exp(scores - top_score)  27.2 us
  transfers between devices with their start and end apart: 23, of which 15 were waited for; matrix products, arithmetic and copies ran while one was open for 13% of the time, Pallas kernels for 0%

profile of v1, /device:TPU:0, one launch (start us, length us, event | category | flops | bytes accessed | tf_op | source)
XLA Modules:
  0.0 805.9 jit_solution(1265749187149874717)
XLA Ops:
  8.6 5.0 collective-permute-start.1
  13.6 21.2 %all_gather.11 = bf16[768,384]{1,0:T(8,128)(2,1)S(1)} all-gather(bf16[48,384]{1,0:T(8,128)(2,1)} %param.26), channel_id=1, replica_groups=mesh['dp'=16,'head'=2] {'dp'}, dimensions={0}, use_global_device_ids=true | all-gather | bytes 626688 | tf_op jit(solution)/shard_map/all_gather | solution.py:92
  41.8 19.0 %all_gather.10 = bf16[768,384]{1,0:T(8,128)(2,1)S(1)} all-gather(bf16[48,384]{1,0:T(8,128)(2,1)S(1)} %copy-done.103), channel_id=1, replica_groups=mesh['dp'=16,'head'=2] {'dp'}, dimensions={0}, use_global_device_ids=true | all-gather | bytes 626688 | tf_op jit(solution)/shard_map/all_gather | solution.py:94
  68.1 21.8 %all_gather.12 = bf16[384,768]{0,1:T(8,128)(2,1)} all-gather(bf16[384,48]{0,1:T(8,128)(2,1)S(1)} %copy-done.104), channel_id=1, replica_groups=mesh['dp'=16,'head'=2] {'dp'}, dimensions={1}, use_global_device_ids=true | all-gather | bytes 626688 | tf_op jit(solution)/shard_map/all_gather | solution.py:98
  108.0 4.1 collective-permute-start.3
  114.8 4.4 collective-permute-start.5
  120.9 4.5 collective-permute-start.7
  127.0 4.5 collective-permute-start.9
  133.1 4.4 collective-permute-start.11
  139.2 4.5 collective-permute-start.13
  146.7 4.8 collective-permute-done.14
  156.9 6.8 fusion.448
  163.7 3.5 fusion.172
  168.7 6.7 fusion.447
  175.4 3.5 fusion.190
  202.4 6.8 fusion.449
  209.3 4.8 fusion.184
  214.0 15.6 %all-reduce.24.cloned.1.call-done = (bf16[512,768]{1,0:T(8,128)(2,1)}, bf16[512,768]{1,0:T(8,128)(2,1)}) async-done(((bf16[512,768]{1,0:T(8,128)(2,1)}, bf16[512,768]{1,0:T(8,128)(2,1)}), (bf16[512,768]{1,0:T(8,128)(2,1)}, bf16[512,768]{1,0:T(8,128)(2,1)})) %all-reduce.24.cloned.1.call-update) | async-done | bytes 1572880 | tf_op jit(solution)/shard_map/psum | solution.py:225
  234.0 5.3 convolution_add_fusion.3
  239.3 3.4 convolution_add_fusion
  242.7 24.4 %all-gather.5.cloned.1.call-done = bf16[1536,768]{0,1:T(8,128)(2,1)} async-done(((bf16[1536,48]{0,1:T(8,128)(2,1)}), bf16[1536,768]{0,1:T(8,128)(2,1)}) %all-gather.5.cloned.1.call-update) | async-done | bytes 2359312 | tf_op jit(solution)/shard_map/all_gather | solution.py:99
  267.1 11.2 %fusion.132 = bf16[512,768]{1,0:T(8,128)(2,1)} fusion(bf16[1536,768]{0,1:T(8,128)(2,1)} %all-gather.5.cloned.1.call-done, f32[512,1536]{1,0:T(8,128)} %convolution_add_fusion.3), kind=kOutput, calls=%fused_computation.254 | convolution fusion | flops 1259470848 | bytes 6291456 | tf_op jit(solution)/shard_map/dot_general | solution.py:44
  278.3 8.8 %fusion.141 = bf16[512,768]{1,0:T(8,128)(2,1)} fusion(bf16[1536,768]{0,1:T(8,128)(2,1)S(1)} %copy-done.154, f32[512,1536]{1,0:T(8,128)S(1)} %copy-done.156), kind=kOutput, calls=%fused_computation.257 | convolution fusion | flops 1259470848 | bytes 6291456 | tf_op jit(solution)/shard_map/dot_general | solution.py:44
  290.1 6.9 fusion.450
  297.0 3.6 fusion.178
  302.2 35.3 %all-reduce.22.cloned.1.call-done = (bf16[512,768]{1,0:T(8,128)(2,1)}, bf16[512,768]{1,0:T(8,128)(2,1)}) async-done(((bf16[512,768]{1,0:T(8,128)(2,1)}, bf16[512,768]{1,0:T(8,128)(2,1)}), (bf16[512,768]{1,0:T(8,128)(2,1)}, bf16[512,768]{1,0:T(8,128)(2,1)})) %all-reduce.22.cloned.1.call-update) | async-done | bytes 1572880 | tf_op jit(solution)/shard_map/psum | solution.py:234
  346.9 7.4 convolution_convert_fusion
  354.3 7.4 convolution_convert_fusion.3
  362.1 86.0 %all-reduce.20.cloned.1.call-done = (bf16[512,768]{1,0:T(8,128)(2,1)}, bf16[512,768]{1,0:T(8,128)(2,1)}, bf16[512,768]{1,0:T(8,128)(2,1)}, bf16[512,768]{1,0:T(8,128)(2,1)}) async-done(((bf16[512,768]{1,0:T(8,128)(2,1)}, bf16[512,768]{1,0:T(8,128)(2,1)}, bf16[512,768]{1,0:T(8,128)(2,1)}, bf16[512,768]{1,0:T(8,128)(2,1)}), (bf16[512,768]{1,0:T(8,128)(2,1)}, bf16[512,768]{1,0:T(8,128)(2,1)}, ...) | async-done | bytes 3145744 | tf_op jit(solution)/shard_map/psum | solution.py:225
  448.2 4.4 multiply_reduce_fusion.7
  456.0 8.8 %fusion.135 = bf16[512,768]{1,0:T(8,128)(2,1)} fusion(bf16[1536,768]{0,1:T(8,128)(2,1)S(1)} %copy-done.155, f32[512,1536]{1,0:T(8,128)S(1)} %convolution_add_fusion.2), kind=kOutput, calls=%fused_computation.255 | convolution fusion | flops 1259470848 | bytes 6291456 | tf_op jit(solution)/shard_map/dot_general | solution.py:44
  468.0 9.0 %fusion.138 = bf16[512,768]{1,0:T(8,128)(2,1)} fusion(bf16[1536,768]{0,1:T(8,128)(2,1)S(1)} %copy-done.155, f32[512,1536]{1,0:T(8,128)S(1)} %convolution_add_fusion.1), kind=kOutput, calls=%fused_computation.256 | convolution fusion | flops 1259470848 | bytes 6291456 | tf_op jit(solution)/shard_map/dot_general | solution.py:44
  477.1 51.8 %all-reduce.18.cloned.1.call-done = (bf16[512,768]{1,0:T(8,128)(2,1)}, bf16[512,768]{1,0:T(8,128)(2,1)}) async-done(((bf16[512,768]{1,0:T(8,128)(2,1)}, bf16[512,768]{1,0:T(8,128)(2,1)}), (bf16[512,768]{1,0:T(8,128)(2,1)}, bf16[512,768]{1,0:T(8,128)(2,1)})) %all-reduce.18.cloned.1.call-update) | async-done | bytes 1572880 | tf_op jit(solution)/shard_map/psum | solution.py:234
  538.1 7.4 convolution_convert_fusion.1
  545.5 7.4 convolution_convert_fusion.2
  553.0 51.7 %all-reduce.16.cloned.1.call-done = (bf16[512,768]{1,0:T(8,128)(2,1)}, bf16[512,768]{1,0:T(8,128)(2,1)}) async-done(((bf16[512,768]{1,0:T(8,128)(2,1)}, bf16[512,768]{1,0:T(8,128)(2,1)}), (bf16[512,768]{1,0:T(8,128)(2,1)}, bf16[512,768]{1,0:T(8,128)(2,1)})) %all-reduce.16.cloned.1.call-update) | async-done | bytes 1572880 | tf_op jit(solution)/shard_map/psum | solution.py:247
  604.8 4.0 multiply_reduce_fusion.6
  609.0 3.1 subtract_multiply_fusion.3
  615.0 3.7 multiply_reduce_fusion.3
  621.2 4.8 multiply_reduce_fusion.2
  631.8 3.7 multiply_reduce_fusion.1
  638.0 3.7 multiply_reduce_fusion
  641.7 3.9 multiply_convert_fusion.3
  653.3 6.6 multiply_convert_fusion.2
  669.6 3.8 multiply_convert_fusion.1
  680.8 3.9 multiply_convert_fusion
  713.1 61.2 %all-reduce = (f32[8,384]{1,0:T(8,128)}, f32[8,384]{1,0:T(8,128)}) all-reduce(f32[8,384]{1,0:T(8,128)S(1)} %fusion.201, f32[8,384]{1,0:T(8,128)S(1)} %fusion.200), channel_id=1, replica_groups=mesh['dp'=16,'head'=2] {'dp'}, use_global_device_ids=true, to_apply=%region_60.61 | all-reduce | flops 6144 | bytes 49152 | tf_op jit(solution)/shard_map/psum | solution.py:113
  774.3 18.6 %all-reduce.14.cloned.1.call-done = (bf16[512,768]{1,0:T(8,128)(2,1)}, bf16[512,768]{1,0:T(8,128)(2,1)}, bf16[512,768]{1,0:T(8,128)(2,1)}, bf16[512,768]{1,0:T(8,128)(2,1)}) async-done(((bf16[512,768]{1,0:T(8,128)(2,1)}, bf16[512,768]{1,0:T(8,128)(2,1)}, bf16[512,768]{1,0:T(8,128)(2,1)}, bf16[512,768]{1,0:T(8,128)(2,1)}), (bf16[512,768]{1,0:T(8,128)(2,1)}, bf16[512,768]{1,0:T(8,128)(2,1)}, ...) | async-done | bytes 3145744 | tf_op jit(solution)/shard_map/psum | solution.py:293
  (556 shorter events, 178.1 us)
Async XLA Ops:
  8.0 32.5 %copy-start = (bf16[768,8]{0,1:T(8,128)(2,1)S(1)}, bf16[768,8]{0,1:T(8,128)(2,1)}, u32[]{:S(2)}) copy-start(bf16[768,8]{0,1:T(8,128)(2,1)} %param.41) | copy-start | bytes 36868
  8.0 32.5 %copy-start.1 = (bf16[4,512,768]{2,1,0:T(8,128)(2,1)S(1)}, bf16[4,512,768]{2,1,0:T(8,128)(2,1)}, u32[]{:S(2)}) copy-start(bf16[4,512,768]{2,1,0:T(8,128)(2,1)} %param.23) | copy-start | bytes 9437188
  8.0 221.6 %all-reduce.24.cloned.1.call-start = ((), (), s32[]{:S(2)}) async-start(), calls=%async_computation.7 | async-start | bytes 3145728 | tf_op jit(solution)/shard_map/psum | solution.py:225
  8.1 99.5 %collective-permute-start = (bf16[48,384]{1,0:T(8,128)(2,1)}, bf16[48,384]{1,0:T(8,128)(2,1)}, u32[]{:S(2)}, u32[]{:S(2)}) collective-permute-start(bf16[48,384]{1,0:T(8,128)(2,1)} %param.27), channel_id=1, source_target_pairs={{0,2},{2,4},{4,6},{6,8},{8,10},{10,12},{12,14},{14,16},{16,18},{18... | collective-permute-start | bytes 110600 | tf_op jit(solution)/shard_map/ppermute | solution.py:25
  8.6 99.4 %collective-permute-start.1 = (bf16[48,384]{1,0:T(8,128)(2,1)}, bf16[48,384]{1,0:T(8,128)(2,1)}, u32[]{:S(2)}, u32[]{:S(2)}) collective-permute-start(bf16[48,384]{1,0:T(8,128)(2,1)} %param.27), channel_id=1, source_target_pairs={{0,30},{2,0},{4,2},{6,4},{8,6},{10,8},{12,10},{14,12},{16,14},{18,... | collective-permute-start | bytes 110600 | tf_op jit(solution)/shard_map/ppermute | solution.py:33
  35.5 25.4 %copy-start.151 = (bf16[384]{0:T(512)(128)(2,1)S(1)}, bf16[384]{0:T(512)(128)(2,1)}, u32[]{:S(2)}) copy-start(bf16[384]{0:T(512)(128)(2,1)} %param.33) | copy-start | bytes 2308
  40.8 56.3 %copy-start.105 = (bf16[512,8]{0,1:T(8,128)(2,1)}, bf16[512,8]{0,1:T(8,128)(2,1)S(1)}, u32[]{:S(2)}) copy-start(bf16[512,8]{0,1:T(8,128)(2,1)S(1)} %convolution_convert_fusion.22) | copy-start | bytes 24580
  40.8 22.8 %copy-start.91 = (bf16[768,8]{0,1:T(8,128)(2,1)S(1)}, bf16[768,8]{0,1:T(8,128)(2,1)}, u32[]{:S(2)}) copy-start(bf16[768,8]{0,1:T(8,128)(2,1)} %param.42) | copy-start | bytes 36868
  62.3 34.8 %copy-start.77 = (f32[8,384]{1,0:T(8,128)S(1)}, f32[8,384]{1,0:T(8,128)}, u32[]{:S(2)}) copy-start(f32[8,384]{1,0:T(8,128)} %param.43) | copy-start | bytes 36868
  91.1 12.2 %copy-start.72 = (f32[512,384]{0,1:T(8,128)S(1)}, f32[512,384]{0,1:T(8,128)}, u32[]{:S(2)}) copy-start(f32[512,384]{0,1:T(8,128)} %convolution_add_fusion.5) | copy-start | bytes 2359300
  91.1 12.2 %copy-start.109 = (bf16[512,8]{0,1:T(8,128)(2,1)S(1)}, bf16[512,8]{0,1:T(8,128)(2,1)}, u32[]{:S(2)}) copy-start(bf16[512,8]{0,1:T(8,128)(2,1)} %convolution_convert_fusion.17) | copy-start | bytes 24580
  101.2 67.5 %copy-start.59 = (bf16[512,384]{0,1:T(8,128)(2,1)}, bf16[512,384]{0,1:T(8,128)(2,1)S(1)}, u32[]{:S(2)}) copy-start(bf16[512,384]{0,1:T(8,128)(2,1)S(1)} %fusion.171) | copy-start | bytes 1179652
  107.6 7.2 collective-permute-start.2
  108.0 6.9 collective-permute-start.3
  114.8 6.1 collective-permute-start.4
  114.8 6.1 collective-permute-start.5
  120.9 6.1 collective-permute-start.6
  120.9 6.1 collective-permute-start.7
  127.0 6.1 collective-permute-start.8
  127.0 6.1 collective-permute-start.9
  133.1 6.1 collective-permute-start.10
  133.1 6.1 collective-permute-start.11
  139.2 6.1 collective-permute-start.12
  139.2 6.9 collective-permute-start.13
  145.2 6.4 collective-permute-start.14
  180.6 53.4 %all-gather.3.cloned.1.call-start = ((), (), s32[]{:S(2)}) async-start(), calls=%async_computation | async-start | bytes 2506752 | tf_op jit(solution)/shard_map/all_gather | solution.py:95
  181.1 86.0 %all-gather.5.cloned.1.call-start = ((), (), s32[]{:S(2)}) async-start(), calls=%async_computation.1 | async-start | bytes 2506752 | tf_op jit(solution)/shard_map/all_gather | solution.py:99
  181.7 155.8 %all-reduce.22.cloned.1.call-start = ((), (), s32[]{:S(2)}) async-start(), calls=%async_computation.6 | async-start | bytes 3145728 | tf_op jit(solution)/shard_map/psum | solution.py:234
  187.7 12.4 %copy-start.117 = (bf16[512,8]{0,1:T(8,128)(2,1)}, bf16[512,8]{0,1:T(8,128)(2,1)S(1)}, u32[]{:S(2)}) copy-start(bf16[512,8]{0,1:T(8,128)(2,1)S(1)} %convolution_convert_fusion.21) | copy-start | bytes 24580
  267.1 11.2 %copy-start.154 = (bf16[1536,768]{0,1:T(8,128)(2,1)S(1)}, bf16[1536,768]{0,1:T(8,128)(2,1)}, u32[]{:S(2)}) copy-start(bf16[1536,768]{0,1:T(8,128)(2,1)} %all-gather.5.cloned.1.call-done) | copy-start | bytes 7077892
  267.1 11.2 %copy-start.156 = (f32[512,1536]{1,0:T(8,128)S(1)}, f32[512,1536]{1,0:T(8,128)}, u32[]{:S(2)}) copy-start(f32[512,1536]{1,0:T(8,128)} %convolution_add_fusion) | copy-start | bytes 9437188
  287.2 161.0 %all-reduce.20.cloned.1.call-start = ((), (), s32[]{:S(2)}) async-start(), calls=%async_computation.5 | async-start | bytes 6291456 | tf_op jit(solution)/shard_map/psum | solution.py:225
  297.0 40.5 %copy-start.90 = (f32[768]{0:T(1024)S(1)}, f32[768]{0:T(1024)}, u32[]{:S(2)}) copy-start(f32[768]{0:T(1024)} %convert_element_type.633) | copy-start | bytes 9220
  297.0 40.5 %copy-start.96 = (f32[512]{0:T(512)S(1)}, f32[512]{0:T(512)}, u32[]{:S(2)}) copy-start(f32[512]{0:T(512)} %copy-done.95) | copy-start | bytes 6148
  297.0 40.5 %copy-start.98 = (f32[512]{0:T(512)S(1)}, f32[512]{0:T(512)}, u32[]{:S(2)}) copy-start(f32[512]{0:T(512)} %copy-done.97) | copy-start | bytes 6148
  297.0 40.5 %copy-start.101 = (f32[768]{0:T(1024)S(1)}, f32[768]{0:T(1024)}, u32[]{:S(2)}) copy-start(f32[768]{0:T(1024)} %convert_element_type.634) | copy-start | bytes 9220
  297.0 40.5 %copy-start.102 = (f32[768]{0:T(1024)S(1)}, f32[768]{0:T(1024)}, u32[]{:S(2)}) copy-start(f32[768]{0:T(1024)} %convert_element_type.640) | copy-start | bytes 9220
  297.0 40.5 %copy-start.122 = (f32[512]{0:T(512)S(1)}, f32[512]{0:T(512)}, u32[]{:S(2)}) copy-start(f32[512]{0:T(512)} %copy-done.121) | copy-start | bytes 6148
  297.0 40.5 %copy-start.124 = (f32[512]{0:T(512)S(1)}, f32[512]{0:T(512)}, u32[]{:S(2)}) copy-start(f32[512]{0:T(512)} %copy-done.123) | copy-start | bytes 6148
  361.7 167.1 %all-reduce.18.cloned.1.call-start = ((), (), s32[]{:S(2)}) async-start(), calls=%async_computation.4 | async-start | bytes 3145728 | tf_op jit(solution)/shard_map/psum | solution.py:234
  477.0 127.8 %all-reduce.16.cloned.1.call-start = ((), (), s32[]{:S(2)}) async-start(), calls=%async_computation.3 | async-start | bytes 3145728 | tf_op jit(solution)/shard_map/psum | solution.py:247
  552.9 240.0 %all-reduce.14.cloned.1.call-start = ((), (), s32[]{:S(2)}) async-start(), calls=%async_computation.2 | async-start | bytes 6291456 | tf_op jit(solution)/shard_map/psum | solution.py:293
  615.0 37.1 %copy-start.43 = (bf16[6,64,512]{2,1,0:T(8,128)(2,1)}, bf16[6,64,512]{2,1,0:T(8,128)(2,1)S(1)}, u32[]{:S(2)}) copy-start(bf16[6,64,512]{2,1,0:T(8,128)(2,1)S(1)} %fusion.175) | copy-start | bytes 1179652
  619.3 10.6 %slice-start.4 = ((s8[6291456]{0:T(1024)(128)(4,1)}), s8[4194304]{0:T(1024)(128)(4,1)S(1)}, s32[]{:S(2)}) async-start(s8[6291456]{0:T(1024)(128)(4,1)} %bitcast.432), calls=%async_computation.12 | async-start | bytes 8388608
  653.3 16.3 %slice-start.6 = ((s8[6291456]{0:T(1024)(128)(4,1)}), s8[4194304]{0:T(1024)(128)(4,1)S(1)}, s32[]{:S(2)}) async-start(s8[6291456]{0:T(1024)(128)(4,1)} %bitcast.434), calls=%async_computation.14 | async-start | bytes 8388608
  653.3 16.3 %slice-start.7 = ((s8[6291456]{0:T(1024)(128)(4,1)}), s8[2097152]{0:T(1024)(128)(4,1)S(1)}, s32[]{:S(2)}) async-start(s8[6291456]{0:T(1024)(128)(4,1)} %bitcast.434), calls=%async_computation.15 | async-start | bytes 4194304
  711.1 81.8 %copy-start.23 = (f32[512,768]{1,0:T(8,128)S(1)}, f32[512,768]{1,0:T(8,128)}, u32[]{:S(2)}) copy-start(f32[512,768]{1,0:T(8,128)} %copy-done.22) | copy-start | bytes 4718596
  711.3 83.1 %copy-start.21 = (f32[512,768]{1,0:T(8,128)S(1)}, f32[512,768]{1,0:T(8,128)}, u32[]{:S(2)}) copy-start(f32[512,768]{1,0:T(8,128)} %copy-done.20) | copy-start | bytes 4718596
  (144 other events, 570.8 us)
Sparse Core Ops, SparseCore 0:
  180.7 48.9 all-reduce.23
  287.3 50.1 all-reduce.21
  361.8 86.3 all-reduce.19
  477.1 51.6 all-reduce.17
  553.1 51.6 all-reduce.15
  706.5 86.3 all-reduce.13
Sparse Core Ops, SparseCore 1:
  183.6 39.8 all-gather.2
  225.9 41.2 all-gather.4
